TPU v7x, 256 devices: a whole 4x4x8 slice. The times are simulated.
256 devices in a mesh: dp: 4 (over x_hi, core), ctx: 64 (over y, z, x_lo).
Axes of the slice: x: 4 (x_hi: 2, x_lo: 2; x = x_hi * 2 + x_lo), y: 4, z: 8, core: 2. Of those that a mesh axis runs over, the one named last changes fastest.
Arguments:
- frames: bfloat16 [4, 12288, 1024], P('dp', 'ctx'), may hold values from -60 to 60
- lengths: int32 [4], P('dp'), may hold values from 6144 to 12288, as said below
- w_qkv: bfloat16 [1024, 1536], replicated, may hold values from -0.9 to 0.9
- w_out: bfloat16 [512, 1024], replicated, may hold values from -0.25 to 0.25
- w_pw1: bfloat16 [1024, 2048], replicated, may hold values from -0.1875 to 0.1875
- conv_taps: float32 [31, 1024], replicated, may hold values from -1 to 1
- w_pw2: bfloat16 [1024, 1024], replicated, may hold values from -0.1875 to 0.1875
Outputs:
- encoded: bfloat16 [4, 12288, 1024], P('dp', 'ctx')
Inputs may be any that keep to these rules, and one draw needn't show every extreme that they name: `lengths`: the valid frames of a recording are its first ones; some recording has all 12288 frames valid.
All inputs are finite; a program needn't handle non-finite values.
Results may differ from a plain program's by a relative error of at most 0.011.
Values may be sent and summed in bfloat16 or wider, within the bound.
A program may use at most 256 MiB of HBM per device.

v0:
```python
import jax
import jax.numpy as jnp
from jax import lax
from jax.sharding import PartitionSpec as P

HEADS = 8


epsilon = 1e-05
masked_score = -1e30


def padded_2(cells, sides, width):
    for axis, dim in sides:
        count = lax.axis_size(axis)
        ends = count - 1
        head = lax.slice_in_dim(cells, 0, width, axis=dim)
        tail = lax.slice_in_dim(cells, cells.shape[dim] - width, cells.shape[dim], axis=dim)
        cells = jnp.concatenate(
            [
                lax.ppermute(tail, axis, [(i, (i + 1) % count) for i in range(ends)]),
                cells,
                lax.ppermute(head, axis, [((i + 1) % count, i) for i in range(ends)]),
            ],
            axis=dim,
        )
    return cells


def to_bf16(value):
    return lax.optimization_barrier(value.astype(jnp.bfloat16))


def layer_norm(value):
    center = value - jnp.mean(value, axis=-1, keepdims=True)
    spread = jnp.mean(center * center, axis=-1, keepdims=True)
    return center * lax.rsqrt(spread + epsilon)


def depthwise(padded, conv_taps, count):
    total = jnp.zeros((count, padded.shape[1]), jnp.float32)
    for tap_index in range(conv_taps.shape[0]):
        total = total + conv_taps[tap_index] * padded[tap_index : tap_index + count].astype(
            jnp.float32
        )
    return total


def gate_rows(stream_rows, spots, limit, w_pw1):
    gated = jnp.dot(
        to_bf16(layer_norm(stream_rows.astype(jnp.float32))),
        w_pw1,
        preferred_element_type=jnp.float32,
    )
    half_cols = gated.shape[1] // 2
    result = gated[:, :half_cols] * jax.nn.sigmoid(gated[:, half_cols:])
    return to_bf16(jnp.where((spots < limit)[:, None], result, 0.0))


def attend_block(carry, query_heads, key_piece, value_piece, limit):
    run_max, run_sum, run_acc = carry
    count = key_piece.shape[0]
    head_count = query_heads.shape[1]
    head_size = query_heads.shape[2]
    key_heads = key_piece.reshape(count, head_count, head_size)
    value_heads = value_piece.reshape(count, head_count, head_size)
    scores = jnp.einsum("qhd,khd->hqk", query_heads, key_heads, preferred_element_type=jnp.float32)
    live = jnp.arange(count, dtype=jnp.int32) < limit
    masked = jnp.where(live, scores, masked_score)
    new_max = jnp.maximum(run_max, jnp.max(masked, axis=-1))
    weights = jnp.where(live, jnp.exp(masked - new_max[:, :, None]), 0.0)
    scale_old = jnp.exp(run_max - new_max)
    new_sum = jnp.sum(weights, axis=-1)
    product = jnp.einsum(
        "hqk,khd->qhd", to_bf16(weights), value_heads, preferred_element_type=jnp.float32
    )
    new_acc = run_acc * scale_old.T[:, :, None] + product
    return (new_max, new_sum, new_acc)


def per_device(frames, lengths, w_qkv, w_out, w_pw1, conv_taps, w_pw2):
    stream = frames[0]
    frame_rows = stream.shape[0]
    my_index = lax.axis_index("ctx")
    my_start = my_index * frame_rows
    limit = lengths[0]
    positions = my_start + jnp.arange(frame_rows, dtype=jnp.int32)
    valid = positions < limit
    normed = to_bf16(layer_norm(stream.astype(jnp.float32)))
    projected = jnp.dot(normed, w_qkv, preferred_element_type=jnp.float32)
    inner = w_out.shape[0]
    head_size = inner // HEADS
    queries = to_bf16(projected[:, :inner] * head_size ** (-0.5)).reshape(
        frame_rows, HEADS, head_size
    )
    keys = to_bf16(projected[:, inner : 2 * inner])
    values = to_bf16(projected[:, 2 * inner :])
    initial = (
        jnp.full((HEADS, frame_rows), masked_score, jnp.float32),
        jnp.zeros((HEADS, frame_rows), jnp.float32),
        jnp.zeros((frame_rows, HEADS, head_size), jnp.float32),
    )
    run_max, run_sum, run_acc = attend_block(
        initial,
        queries,
        lax.all_gather(keys, "ctx", axis=0, tiled=True),
        lax.all_gather(values, "ctx", axis=0, tiled=True),
        limit,
    )
    attended = to_bf16(run_acc / run_sum.T[:, :, None]).reshape(frame_rows, inner)
    first = to_bf16(
        stream.astype(jnp.float32) + jnp.dot(attended, w_out, preferred_element_type=jnp.float32)
    )
    half_width = conv_taps.shape[0] // 2
    gated_own = gate_rows(first, positions, limit, w_pw1)
    padded = padded_2(gated_own, (("ctx", 0),), half_width)
    conv = depthwise(padded, conv_taps, frame_rows)
    swished = to_bf16(jax.nn.silu(layer_norm(conv)))
    second = first.astype(jnp.float32) + jnp.dot(swished, w_pw2, preferred_element_type=jnp.float32)
    encoded = jnp.where(valid[:, None], layer_norm(second), 0.0).astype(jnp.bfloat16)
    return encoded[None]


def solution(mesh):
    in_specs = (P("dp", "ctx", None), P("dp"), P(), P(), P(), P(), P())
    out_specs = P("dp", "ctx", None)
    return jax.shard_map(
        per_device, mesh=mesh, in_specs=in_specs, out_specs=out_specs, check_vma=False
    )
```

profile of v0, /device:TPU:8, one launch (start us, length us, event | category | flops | bytes accessed | tf_op | source)
XLA Modules:
  0.0 722.8 jit_solution(17029172689337861144)
XLA Ops:
  6.5 1.3 convert_reduce_fusion.1
  7.8 1.2 fusion.13
  9.1 1.2 fusion.14
  10.3 1.9 fusion.56
  12.2 0.8 fusion.52
  13.0 0.7 all-gather.5.cloned.1.call-update
  13.7 1.0 fusion.50
  16.1 1.8 fusion.54
  18.0 308.5 %all-gather.3.cloned.1.call-done = bf16[12288,512]{1,0:T(8,128)(2,1)} async-done(((bf16[192,512]{1,0:T(8,128)(2,1)}), bf16[12288,512]{1,0:T(8,128)(2,1)}) %all-gather.3.cloned.1.call-update) | async-done | bytes 12582928 | tf_op jit(solution)/shard_map/all_gather | solution.py:106
  326.5 16.6 %copy.12 = bf16[12288,512]{0,1:T(8,128)(2,1)} copy(bf16[12288,512]{1,0:T(8,128)(2,1)} %all-gather.3.cloned.1.call-done) | data formatting | bytes 25165824 | tf_op jit(solution)/shard_map/all_gather | solution.py:106
  343.1 30.9 %select_reduce_fusion = (f32[8,192]{1,0:T(8,128)S(1)}, f32[8,192,12288]{2,1,0:T(8,128)}) fusion(pred[12288]{0:T(1024)(128)(4,1)S(1)} %iota_compare_fusion, bf16[192,8,64]{0,2,1:T(8,128)(2,1)S(1)} %bitcast.79, bf16[12288,8,64]{0,2,1:T(8,128)(2,1)} %bitcast.78), kind=kOutput, calls=%fused_computation.1 | convolution fusion | flops 2453666304 | bytes 88295424 | tf_op jit(solution)/shard_map/qhd,khd->hqk/dot_general | solution.py:67
  374.0 37.6 %fusion = (f32[8,192]{1,0:T(8,128)S(1)}, bf16[8,192,12288]{2,1,0:T(8,128)(2,1)}) fusion(f32[8,192,12288]{2,1,0:T(8,128)} %get-tuple-element.49, f32[8,192]{1,0:T(8,128)S(1)} %get-tuple-element.45, pred[12288]{0:T(1024)(128)(4,1)S(1)} %iota_compare_fusion), kind=kLoop, calls=%fused_computation.2 | loop fusion | flops 94370304 | bytes 113270784 | tf_op jit(solution)/shard_map/reduce_sum | solution.py:73
  411.7 241.2 %all-gather.5.cloned.1.call-done = bf16[12288,512]{1,0:T(8,128)(2,1)} async-done(((bf16[192,512]{1,0:T(8,128)(2,1)}), bf16[12288,512]{1,0:T(8,128)(2,1)}) %all-gather.5.cloned.1.call-update) | async-done | bytes 12582928 | tf_op jit(solution)/shard_map/all_gather | solution.py:107
  652.9 16.5 %copy.13 = bf16[12288,512]{0,1:T(8,128)(2,1)} copy(bf16[12288,512]{1,0:T(8,128)(2,1)} %all-gather.5.cloned.1.call-done) | data formatting | bytes 25165824 | tf_op jit(solution)/shard_map/all_gather | solution.py:107
  669.4 21.5 %fusion.5 = bf16[192,8,64]{0,2,1:T(8,128)(2,1)} fusion(bf16[12288,8,64]{0,2,1:T(8,128)(2,1)} %bitcast.77, bf16[8,192,12288]{2,1,0:T(8,128)(2,1)} %get-tuple-element.8, f32[192,8]{0,1:T(8,128)S(1)} %bitcast.81, f32[192,8]{0,1:T(8,128)S(1)} %get-tuple-element.44), kind=kOutput, calls=%fused_computation.38 | convolution fusion | flops 2416214016 | bytes 50540544 | tf_op jit(solution)/shard_map/hqk,khd->qhd/dot_general | solution.py:74
  690.9 1.9 fusion.2
  693.4 3.2 fusion.58
  696.6 0.8 fusion.20
  697.5 1.9 collective-permute-start
  699.4 7.1 collective-permute-start.1
  706.5 1.1 fusion.55
  707.9 5.5 fusion.51
  714.1 0.7 fusion.57
  715.1 0.9 fusion.21
  (34 shorter events, 2.5 us)
Async XLA Ops:
  6.5 3.8 copy-start
  6.5 320.0 %all-gather.3.cloned.1.call-start = ((), (), s32[]{:S(2)}) async-start(), calls=%async_computation | async-start | bytes 12779520 | tf_op jit(solution)/shard_map/all_gather | solution.py:106
  13.0 639.9 %all-gather.5.cloned.1.call-start = ((), (), s32[]{:S(2)}) async-start(), calls=%async_computation.1 | async-start | bytes 12779520 | tf_op jit(solution)/shard_map/all_gather | solution.py:107
  669.4 21.5 %copy-start.2 = (bf16[1,192,1024]{2,1,0:T(8,128)(2,1)S(1)}, bf16[1,192,1024]{2,1,0:T(8,128)(2,1)}, u32[]{:S(2)}) copy-start(bf16[1,192,1024]{2,1,0:T(8,128)(2,1)} %param.7) | copy-start | bytes 1179652
  669.4 46.6 %copy-start.1 = (bf16[1024,1536]{1,0:T(8,128)(2,1)S(1)}, bf16[1024,1536]{1,0:T(8,128)(2,1)}, u32[]{:S(2)}) copy-start(bf16[1024,1536]{1,0:T(8,128)(2,1)} %param.9) | copy-start | bytes 9437188
  690.9 23.2 %copy-start.3 = (bf16[1024,1024]{1,0:T(8,128)(2,1)S(1)}, bf16[1024,1024]{1,0:T(8,128)(2,1)}, u32[]{:S(2)}) copy-start(bf16[1024,1024]{1,0:T(8,128)(2,1)} %param.13) | copy-start | bytes 6291460
  690.9 24.2 %copy-start.4 = (pred[192]{0:T(512)(128)(4,1)S(1)}, pred[192]{0:T(512)(128)(4,1)}, u32[]{:S(2)}) copy-start(pred[192]{0:T(512)(128)(4,1)} %add_compare_fusion) | copy-start | bytes 580
  697.5 10.2 %collective-permute-start = (bf16[15,1024]{1,0:T(8,128)(2,1)S(1)}, bf16[15,1024]{1,0:T(8,128)(2,1)S(1)}, u32[]{:S(2)}, u32[]{:S(2)}) collective-permute-start(bf16[15,1024]{1,0:T(8,128)(2,1)S(1)} %get-tuple-element.11), channel_id=1, source_target_pairs={{0,1},{1,2},{2,3},{3,4},{4,5},{5,6},{6,7},{7,8},{8,9},{9,10},{10,1... | collective-permute-start | bytes 92168 | tf_op jit(solution)/shard_map/ppermute | solution.py:21
  699.4 8.5 %collective-permute-start.1 = (bf16[15,1024]{1,0:T(8,128)(2,1)S(1)}, bf16[15,1024]{1,0:T(8,128)(2,1)S(1)}, u32[]{:S(2)}, u32[]{:S(2)}) collective-permute-start(bf16[15,1024]{1,0:T(8,128)(2,1)S(1)} %get-tuple-element.12), channel_id=1, source_target_pairs={{1,0},{2,1},{3,2},{4,3},{5,4},{6,5},{7,6},{8,7},{9,8},{10,9},{11,1... | collective-permute-start | bytes 92168 | tf_op jit(solution)/shard_map/ppermute | solution.py:23
Sparse Core Ops, SparseCore 0:
  13.1 313.3 all-gather.2
  328.3 324.5 all-gather.4
where the time goes:
time: 737 us; the launch traced here: 723 us
  waiting for transfers between devices  551 us (75%)
  matrix products  60 us (8%)
  other arithmetic  51.8 us (7%)
  local copies, waits for them, and re-layouts  37 us (5%)
  between operations  14.2 us (2%)
  starting transfers between devices  9.08 us (1%)
    all_gather x1, waiting for transfers between devices, per_device(): lax.all_gather(keys, 'ctx', axis=0, tiled=True)  309 us
    all_gather x1, waiting for transfers between devices, per_device(): lax.all_gather(values, 'ctx', axis=0, tiled=True)  241 us
    reduce_sum x1, other arithmetic, attend_block(): new_sum = jnp.sum(weights, axis=-1)  37.6 us
    dot_general x1, matrix products, attend_block(): jnp.einsum('qhd,khd->hqk', query_heads, key_heads, preferred_element_type...  30.9 us
    dot_general x1, matrix products, attend_block(): jnp.einsum('hqk,khd->qhd', to_bf16(weights), value_heads, preferred_eleme...  21.5 us
    all_gather x1, local copies, waits for them, and re-layouts, per_device(): lax.all_gather(keys, 'ctx', axis=0, tiled=True)  16.6 us
    all_gather x1, local copies, waits for them, and re-layouts, per_device(): lax.all_gather(values, 'ctx', axis=0, tiled=True)  16.5 us
  transfers between devices with their start and end apart: 4, of which 3 were waited for; matrix products, arithmetic and copies ran while one was open for 12% of the time, Pallas kernels for 0%

commit v1 on v0

--- a/solution.py
+++ b/solution.py
@@ -1,6 +1,8 @@
 import jax
 import jax.numpy as jnp
 from jax import lax
+from jax.experimental import pallas as pl
+from jax.experimental.pallas import tpu as pltpu
 from jax.sharding import PartitionSpec as P
 
 HEADS = 8
@@ -28,7 +30,7 @@
 
 
 def to_bf16(value):
-    return lax.optimization_barrier(value.astype(jnp.bfloat16))
+    return value.astype(jnp.bfloat16)
 
 
 def layer_norm(value):
@@ -57,25 +59,67 @@
     return to_bf16(jnp.where((spots < limit)[:, None], result, 0.0))
 
 
-def attend_block(carry, query_heads, key_piece, value_piece, limit):
-    run_max, run_sum, run_acc = carry
-    count = key_piece.shape[0]
-    head_count = query_heads.shape[1]
-    head_size = query_heads.shape[2]
-    key_heads = key_piece.reshape(count, head_count, head_size)
-    value_heads = value_piece.reshape(count, head_count, head_size)
-    scores = jnp.einsum("qhd,khd->hqk", query_heads, key_heads, preferred_element_type=jnp.float32)
-    live = jnp.arange(count, dtype=jnp.int32) < limit
-    masked = jnp.where(live, scores, masked_score)
-    new_max = jnp.maximum(run_max, jnp.max(masked, axis=-1))
-    weights = jnp.where(live, jnp.exp(masked - new_max[:, :, None]), 0.0)
-    scale_old = jnp.exp(run_max - new_max)
-    new_sum = jnp.sum(weights, axis=-1)
-    product = jnp.einsum(
-        "hqk,khd->qhd", to_bf16(weights), value_heads, preferred_element_type=jnp.float32
-    )
-    new_acc = run_acc * scale_old.T[:, :, None] + product
-    return (new_max, new_sum, new_acc)
+def attend_kernel(bias_ref, q_ref, kv_ref, out_ref):
+    rows = q_ref.shape[0]
+    inner = q_ref.shape[1]
+    keys = kv_ref.shape[0]
+    bias = bias_ref[...]
+    lane = lax.broadcasted_iota(jnp.int32, (rows, 128), 1)
+    low = lane < 64
+    ones = jnp.ones((keys, 128), jnp.bfloat16)
+    stats = jnp.zeros((rows, 128), jnp.float32)
+    for pair in range(HEADS // 2):
+        cols = slice(pair * 128, pair * 128 + 128)
+        q_pair = q_ref[:, cols]
+        k_pair = kv_ref[:, cols]
+        v_ext = jnp.concatenate(
+            [kv_ref[:, inner + pair * 128 : inner + pair * 128 + 128], ones], axis=1
+        )
+        parts = []
+        for side in range(2):
+            head = 2 * pair + side
+            mine = low if side == 0 else jnp.logical_not(low)
+            q_head = jnp.where(mine, q_pair, jnp.zeros_like(q_pair))
+            scores = lax.dot_general(
+                q_head, k_pair, (((1,), (1,)), ((), ())), preferred_element_type=jnp.float32
+            )
+            scores = scores + bias
+            top = jnp.max(scores, axis=-1, keepdims=True)
+            weights = jnp.exp(scores - top).astype(jnp.bfloat16)
+            product = jnp.dot(weights, v_ext, preferred_element_type=jnp.float32)
+            total = product[:, 128:]
+            parts.append(product[:, :128] / total)
+            lse = top + jnp.log(total)
+            stats = jnp.where((lane & 7) == head, lse, stats)
+        out_ref[:, cols] = jnp.where(low, parts[0], parts[1]).astype(jnp.bfloat16)
+    high = stats.astype(jnp.bfloat16).astype(jnp.float32)
+    rest = stats - high
+    mid = rest.astype(jnp.bfloat16).astype(jnp.float32)
+    packed = jnp.where(lane < 8, high, jnp.where(lane < 16, mid, rest - mid))
+    out_ref[:, inner:] = packed.astype(jnp.bfloat16)
+
+
+def attend(bias, queries, kv):
+    count, inner = queries.shape
+    keys = kv.shape[0]
+    block = 512
+    return pl.pallas_call(
+        attend_kernel,
+        grid=(count // block,),
+        in_specs=[
+            pl.BlockSpec((1, keys), lambda i: (0, 0)),
+            pl.BlockSpec((block, inner), lambda i: (i, 0)),
+            pl.BlockSpec((keys, 2 * inner), lambda i: (0, 0)),
+        ],
+        out_specs=pl.BlockSpec((block, inner + 128), lambda i: (i, 0)),
+        out_shape=jax.ShapeDtypeStruct((count, inner + 128), jnp.bfloat16),
+        compiler_params=pltpu.CompilerParams(vmem_limit_bytes=60 * 1024 * 1024),
+    )(bias, queries, kv)
+
+
+Z_SIZE = 8
+KV_GROUPS = [[y * 16 + z * 2 + x for z in range(8)] for y in range(4) for x in range(2)]
+Q_GROUPS = [[y * 16 + z * 2 + x for y in range(4) for x in range(2)] for z in range(8)]
 
 
 def per_device(frames, lengths, w_qkv, w_out, w_pw1, conv_taps, w_pw2):
@@ -90,24 +134,25 @@
     projected = jnp.dot(normed, w_qkv, preferred_element_type=jnp.float32)
     inner = w_out.shape[0]
     head_size = inner // HEADS
-    queries = to_bf16(projected[:, :inner] * head_size ** (-0.5)).reshape(
-        frame_rows, HEADS, head_size
-    )
-    keys = to_bf16(projected[:, inner : 2 * inner])
-    values = to_bf16(projected[:, 2 * inner :])
-    initial = (
-        jnp.full((HEADS, frame_rows), masked_score, jnp.float32),
-        jnp.zeros((HEADS, frame_rows), jnp.float32),
-        jnp.zeros((frame_rows, HEADS, head_size), jnp.float32),
-    )
-    run_max, run_sum, run_acc = attend_block(
-        initial,
-        queries,
-        lax.all_gather(keys, "ctx", axis=0, tiled=True),
-        lax.all_gather(values, "ctx", axis=0, tiled=True),
-        limit,
-    )
-    attended = to_bf16(run_acc / run_sum.T[:, :, None]).reshape(frame_rows, inner)
+    queries = to_bf16(projected[:, :inner] * head_size ** (-0.5))
+    kv = to_bf16(projected[:, inner:])
+    kv_all = lax.all_gather(kv, "ctx", axis=0, tiled=True, axis_index_groups=KV_GROUPS)
+    q_all = lax.all_gather(queries, "ctx", axis=0, tiled=True, axis_index_groups=Q_GROUPS)
+    group_start = (my_index // 16) * 16 + my_index % 2
+    key_rows = jnp.arange(Z_SIZE * frame_rows, dtype=jnp.int32)
+    key_spots = (group_start + 2 * (key_rows // frame_rows)) * frame_rows + key_rows % frame_rows
+    bias = jnp.where(key_spots < limit, 0.0, masked_score).astype(jnp.float32)[None]
+    partial = attend(bias, q_all, kv_all)
+    width = partial.shape[1]
+    returned = lax.all_to_all(
+        partial, "ctx", split_axis=0, concat_axis=0, tiled=True, axis_index_groups=Q_GROUPS
+    ).reshape(8, frame_rows, width)
+    stats = returned[:, :, inner : inner + 24].astype(jnp.float32)
+    lse = stats[:, :, 0:8] + stats[:, :, 8:16] + stats[:, :, 16:24]
+    share = jnp.exp(lse - jnp.max(lse, axis=0))
+    share = share / jnp.sum(share, axis=0)
+    share = jnp.repeat(share, head_size, axis=2)
+    attended = to_bf16(jnp.sum(returned[:, :, :inner].astype(jnp.float32) * share, axis=0))
     first = to_bf16(
         stream.astype(jnp.float32) + jnp.dot(attended, w_out, preferred_element_type=jnp.float32)
     )

time: 737 us -> 207 us (0.28); the launches traced: 723 us -> 207 us
  waiting for transfers between devices: 551 us -> 117 us
  matrix products: 60 us -> 5.46 us
  other arithmetic: 51.8 us -> 15.2 us
  Pallas kernels: 0 us -> 28.9 us
  local copies, waits for them, and re-layouts: 37 us -> 10.9 us
    all_gather x2, waiting for transfers between devices: 550 us -> 92 us  [the longest x1 48.1 us: per_device(): lax.all_gather(kv, 'ctx', axis=0, tiled=True, axis_index_groups=KV_GROUPS)]
    dot_general x2 -> x0, matrix products: 52.4 us -> none  [the longest x1 30.9 us: attend_block(): jnp.einsum('qhd,khd->hqk', query_heads, key_heads, preferred_element_type...]
    reduce_sum x1 -> x2, other arithmetic: 37.6 us -> 2.36 us  [the longest x1 2.22 us: per_device(): jnp.sum(returned[:, :, :inner].astype(jnp.float32) * share, axis=0)]
    all_gather x2 -> x0, local copies, waits for them, and re-layouts: 33.1 us -> none  [the longest x1 16.6 us: per_device(): lax.all_gather(keys, 'ctx', axis=0, tiled=True)]
    pallas_call x0 -> x1, Pallas kernels: none -> 28.9 us  [attend(): pl.pallas_call(attend_kernel, grid=(count // block,), in_specs=[pl.BlockS...]
    all_to_all x0 -> x1, waiting for transfers between devices: none -> 23.6 us  [per_device(): lax.all_to_all(partial, 'ctx', split_axis=0, concat_axis=0, tiled=True, a...]
  transfers between devices with their start and end apart: 4 -> 5, of which waited for: 3 -> 4; matrix products, arithmetic and copies ran while one was open for 12% -> 1% of each run, Pallas kernels for 0% -> 0%
where the time goes in v1:
time: 207 us
  waiting for transfers between devices  117 us (57%)
  Pallas kernels  28.9 us (14%)
  other arithmetic  15.2 us (7%)
  starting transfers between devices  14.9 us (7%)
  between operations  14.3 us (7%)
  local copies, waits for them, and re-layouts  10.9 us (5%)
  matrix products  5.46 us (3%)
    all_gather x1, waiting for transfers between devices, per_device(): lax.all_gather(kv, 'ctx', axis=0, tiled=True, axis_index_groups=KV_GROUPS)  48.1 us
    all_gather x1, waiting for transfers between devices, per_device(): lax.all_gather(queries, 'ctx', axis=0, tiled=True, axis_index_groups=Q_GR...  43.9 us
    pallas_call x1, Pallas kernels, attend(): pl.pallas_call(attend_kernel, grid=(count // block,), in_specs=[pl.BlockS...  28.9 us
    all_to_all x1, waiting for transfers between devices, per_device(): lax.all_to_all(partial, 'ctx', split_axis=0, concat_axis=0, tiled=True, a...  23.6 us
    all_to_all x1, starting transfers between devices, per_device(): lax.all_to_all(partial, 'ctx', split_axis=0, concat_axis=0, tiled=True, a...  5.86 us
    ppermute x1, starting transfers between devices, padded_2(): lax.ppermute(head, axis, [((i + 1) % count, i) for i in range(ends)])  5.82 us
    reduce_sum x2, other arithmetic, layer_norm(): center = value - jnp.mean(value, axis=-1, keepdims=True)  5.78 us
    unnamed x13, local copies, waits for them, and re-layouts  4.74 us
  transfers between devices with their start and end apart: 5, of which 4 were waited for; matrix products, arithmetic and copies ran while one was open for 1% of the time, Pallas kernels for 0%

profile of v1, /device:TPU:8, one launch (start us, length us, event | category | flops | bytes accessed | tf_op | source)
XLA Modules:
  0.0 206.6 jit_solution(18206756797617525838)
XLA Ops:
  6.5 1.3 convert_reduce_fusion
  7.8 1.2 fusion.6
  9.1 1.8 fusion.18
  11.0 1.0 copy-done.3
  12.7 1.9 slice.616
  16.0 43.9 %all-gather.3.cloned.1.call-done.q_ref = bf16[1536,512]{1,0:T(8,128)(2,1)} async-done(((bf16[192,512]{1,0:T(8,128)(2,1)}), bf16[1536,512]{1,0:T(8,128)(2,1)}) %all-gather.3.cloned.1.call-update) | async-done | bytes 1572880 | tf_op jit(solution)/shard_map/all_gather | solution.py:140
  59.9 48.1 %all-gather.5.cloned.1.call-done.kv_ref = bf16[1536,1024]{1,0:T(8,128)(2,1)} async-done(((bf16[192,1024]{1,0:T(8,128)(2,1)}), bf16[1536,1024]{1,0:T(8,128)(2,1)}) %all-gather.5.cloned.1.call-update) | async-done | bytes 3145744 | tf_op jit(solution)/shard_map/all_gather | solution.py:139
  108.0 28.9 %shard_map.73 = bf16[1536,640]{1,0:T(8,128)(2,1)} custom-call(f32[1,1536]{1,0:T(1,128)} %compare_select_fusion.bias_ref, bf16[1536,512]{1,0:T(8,128)(2,1)} %all-gather.3.cloned.1.call-done.q_ref, bf16[1536,1024]{1,0:T(8,128)(2,1)} %all-gather.5.cloned.1.call-done.kv_ref), custom_call_target="tpu_custom_call" | custom-call | tf_op jit(solution)/shard_map/pallas_call | solution.py:106
  136.8 5.9 %all-to-all-start = ((bf16[8,192,640]{2,1,0:T(8,128)(2,1)}), bf16[8,192,640]{2,1,0:T(8,128)(2,1)}, u32[]{:S(2)}, u32[]{:S(2)}) async-start(bf16[8,192,640]{2,1,0:T(8,128)(2,1)} %bitcast.61), calls=%async_computation | async-start | bytes 3932160 | tf_op jit(solution)/shard_map/all_to_all | solution.py:147
  142.8 23.6 %all-to-all-done = bf16[8,192,640]{2,1,0:T(8,128)(2,1)} async-done(((bf16[8,192,640]{2,1,0:T(8,128)(2,1)}), bf16[8,192,640]{2,1,0:T(8,128)(2,1)}, u32[]{:S(2)}, u32[]{:S(2)}) %all-to-all-start) | async-done | bytes 1966112 | tf_op jit(solution)/shard_map/all_to_all | solution.py:147
  166.4 1.0 slice_convert_fusion.1
  168.0 1.0 fusion.14
  169.1 1.4 copy.10
  170.5 2.7 %slice.321 = bf16[8,192,512]{2,1,0:T(8,128)(2,1)} slice(bf16[8,192,640]{2,1,0:T(8,128)(2,1)} %all-to-all-done), slice={[0:8], [0:192], [0:512]} | slice | bytes 3145728 | tf_op jit(solution)/shard_map/slice | solution.py:155
  173.1 3.7 %copy.11 = bf16[8,192,512]{1,2,0:T(8,128)(2,1)} copy(bf16[8,192,512]{2,1,0:T(8,128)(2,1)} %slice.321) | data formatting | bytes 3145728
  176.9 2.2 %fusion = bf16[192,512]{0,1:T(8,128)(2,1)S(1)} fusion(bf16[8,192,512]{1,2,0:T(8,128)(2,1)} %copy.11, f32[8,192,8]{1,2,0:T(8,128)S(1)} %copy.10), kind=kLoop, calls=%fused_computation.1 | loop fusion | flops 2260992 | bytes 1818624 | tf_op jit(solution)/shard_map/reduce_sum | solution.py:155
  179.1 1.7 fusion.67
  181.1 1.1 fusion.16
  182.4 3.2 %collective-permute-start = (bf16[15,1024]{1,0:T(8,128)(2,1)S(1)}, bf16[15,1024]{1,0:T(8,128)(2,1)S(1)}, u32[]{:S(2)}, u32[]{:S(2)}) collective-permute-start(bf16[15,1024]{1,0:T(8,128)(2,1)S(1)} %get-tuple-element.9), channel_id=1, source_target_pairs={{0,1},{1,2},{2,3},{3,4},{4,5},{5,6},{6,7},{7,8},{8,9},{9,10},{10,1... | collective-permute-start | bytes 92168 | tf_op jit(solution)/shard_map/ppermute | solution.py:23
  185.6 5.8 %collective-permute-start.1 = (bf16[15,1024]{1,0:T(8,128)(2,1)S(1)}, bf16[15,1024]{1,0:T(8,128)(2,1)S(1)}, u32[]{:S(2)}, u32[]{:S(2)}) collective-permute-start(bf16[15,1024]{1,0:T(8,128)(2,1)S(1)} %get-tuple-element.10), channel_id=1, source_target_pairs={{1,0},{2,1},{3,2},{4,3},{5,4},{6,5},{7,6},{8,7},{9,8},{10,9},{11,1... | collective-permute-start | bytes 92168 | tf_op jit(solution)/shard_map/ppermute | solution.py:25
  191.5 1.5 collective-permute-done.1
  193.0 4.5 %fusion.62 = (f32[192]{0:T(256)S(1)}, f32[192,1024]{1,0:T(8,128)S(1)}) fusion(bf16[15,1024]{1,0:T(8,128)(2,1)S(1)} %collective-permute-done.1, bf16[192,1024]{1,0:T(8,128)(2,1)S(1)} %fusion.13, f32[1024]{0:T(1024)S(1)} %bitcast.91, f32[1024]{0:T(1024)S(1)} %bitcast.92, f32[1024]{0:T(1024)S(1)} %bitcast.63, f32[1024]{0:T(1024)S(1)} %bitcast.64, ...), kind=kLoop, calls=%fused_computation.143 | loop fusion | flops 35979072 | bytes 1368832 | tf_op jit(solution)/shard_map/reduce_sum | solution.py:37
  197.8 0.8 fusion.68
  198.9 0.9 fusion.17
  (36 shorter events, 3.1 us)
Async XLA Ops:
  6.5 2.5 %copy-start = (bf16[1024,1536]{1,0:T(8,128)(2,1)S(1)}, bf16[1024,1536]{1,0:T(8,128)(2,1)}, u32[]{:S(2)}) copy-start(bf16[1024,1536]{1,0:T(8,128)(2,1)} %param.9) | copy-start | bytes 9437188
  6.5 53.4 %all-gather.3.cloned.1.call-start = ((), (), s32[]{:S(2)}) async-start(), calls=%async_computation.1 | async-start | bytes 1769472 | tf_op jit(solution)/shard_map/all_gather | solution.py:140
  10.9 1.0 copy-start.3
  12.7 95.3 %all-gather.5.cloned.1.call-start = ((), (), s32[]{:S(2)}) async-start(), calls=%async_computation.2 | async-start | bytes 3538944 | tf_op jit(solution)/shard_map/all_gather | solution.py:139
  136.8 5.9 %copy-start.4 = (f32[31,1024]{1,0:T(8,128)S(1)}, f32[31,1024]{1,0:T(8,128)}, u32[]{:S(2)}) copy-start(f32[31,1024]{1,0:T(8,128)} %param.12) | copy-start | bytes 380932
  136.8 29.5 %all-to-all-start = ((bf16[8,192,640]{2,1,0:T(8,128)(2,1)}), bf16[8,192,640]{2,1,0:T(8,128)(2,1)}, u32[]{:S(2)}, u32[]{:S(2)}) async-start(bf16[8,192,640]{2,1,0:T(8,128)(2,1)} %bitcast.61), calls=%async_computation | async-start | bytes 3932160 | tf_op jit(solution)/shard_map/all_to_all | solution.py:147
  176.9 2.2 %copy-start.1 = (bf16[1,192,1024]{2,1,0:T(8,128)(2,1)S(1)}, bf16[1,192,1024]{2,1,0:T(8,128)(2,1)}, u32[]{:S(2)}) copy-start(bf16[1,192,1024]{2,1,0:T(8,128)(2,1)} %param.7) | copy-start | bytes 1179652
  176.9 4.2 %copy-start.2 = (bf16[1024,2048]{1,0:T(8,128)(2,1)S(1)}, bf16[1024,2048]{1,0:T(8,128)(2,1)}, u32[]{:S(2)}) copy-start(bf16[1024,2048]{1,0:T(8,128)(2,1)} %param.11) | copy-start | bytes 12582916
  182.2 15.6 %copy-start.5 = (bf16[1024,1024]{1,0:T(8,128)(2,1)S(1)}, bf16[1024,1024]{1,0:T(8,128)(2,1)}, u32[]{:S(2)}) copy-start(bf16[1024,1024]{1,0:T(8,128)(2,1)} %param.13) | copy-start | bytes 6291460
  182.4 9.0 %collective-permute-start = (bf16[15,1024]{1,0:T(8,128)(2,1)S(1)}, bf16[15,1024]{1,0:T(8,128)(2,1)S(1)}, u32[]{:S(2)}, u32[]{:S(2)}) collective-permute-start(bf16[15,1024]{1,0:T(8,128)(2,1)S(1)} %get-tuple-element.9), channel_id=1, source_target_pairs={{0,1},{1,2},{2,3},{3,4},{4,5},{5,6},{6,7},{7,8},{8,9},{9,10},{10,1... | collective-permute-start | bytes 92168 | tf_op jit(solution)/shard_map/ppermute | solution.py:23
  185.6 7.4 %collective-permute-start.1 = (bf16[15,1024]{1,0:T(8,128)(2,1)S(1)}, bf16[15,1024]{1,0:T(8,128)(2,1)S(1)}, u32[]{:S(2)}, u32[]{:S(2)}) collective-permute-start(bf16[15,1024]{1,0:T(8,128)(2,1)S(1)} %get-tuple-element.10), channel_id=1, source_target_pairs={{1,0},{2,1},{3,2},{4,3},{5,4},{6,5},{7,6},{8,7},{9,8},{10,9},{11,1... | collective-permute-start | bytes 92168 | tf_op jit(solution)/shard_map/ppermute | solution.py:25
Sparse Core Ops, SparseCore 0:
  12.8 47.0 all-gather.2
  61.7 46.2 all-gather.4

commit v2 on v1

--- a/solution.py
+++ b/solution.py
@@ -117,8 +117,105 @@
     )(bias, queries, kv)
 
 
+def gather_kernel(q_ref, kv_ref, q_all, kv_all, q_send, q_recv, kv_send, kv_recv, own_sem):
+    me = lax.axis_index("ctx")
+    y, z, x = me // 16, (me // 2) % 8, me % 2
+    mine = y * 2 + x
+    rows = q_ref.shape[0]
+    half = rows // 2
+
+    def ring_peer(shift):
+        return y * 16 + lax.rem(z + shift + 8, 8) * 2 + x
+
+    def plane_peer(shift):
+        spot = lax.rem(mine + shift, 8)
+        return (spot // 2) * 16 + z * 2 + lax.rem(spot, 2)
+
+    barrier = pltpu.get_barrier_semaphore()
+    for peer in [ring_peer(1), ring_peer(-1)] + [plane_peer(j) for j in range(1, 8)]:
+        pl.semaphore_signal(
+            barrier, inc=1, device_id={"ctx": peer}, device_id_type=pl.DeviceIdType.MESH
+        )
+    pl.semaphore_wait(barrier, 9)
+
+    def ring_copy(way, step, chunk):
+        sign = 1 if way == 0 else -1
+        slot = lax.rem(z - sign * (step - 1) + 8, 8)
+        place = pl.ds(pl.multiple_of(slot * rows + chunk * half, half), half)
+        source = kv_ref.at[pl.ds(chunk * half, half)] if step == 1 else kv_all.at[place]
+        return pltpu.make_async_remote_copy(
+            src_ref=source,
+            dst_ref=kv_all.at[place],
+            send_sem=kv_send.at[way, step - 1, chunk],
+            recv_sem=kv_recv.at[way, step - 1, chunk],
+            device_id={"ctx": ring_peer(sign)},
+            device_id_type=pl.DeviceIdType.MESH,
+        )
+
+    ring = {}
+    for chunk in range(2):
+        for way in range(2):
+            ring[way, 1, chunk] = ring_copy(way, 1, chunk)
+            ring[way, 1, chunk].start()
+    pushes = []
+    q_place = pl.ds(pl.multiple_of(mine * rows, rows), rows)
+    for j in range(1, 8):
+        push = pltpu.make_async_remote_copy(
+            src_ref=q_ref,
+            dst_ref=q_all.at[q_place],
+            send_sem=q_send.at[j],
+            recv_sem=q_recv.at[j],
+            device_id={"ctx": plane_peer(j)},
+            device_id_type=pl.DeviceIdType.MESH,
+        )
+        push.start()
+        pushes.append(push)
+    own_q = pltpu.make_async_copy(q_ref, q_all.at[q_place], own_sem.at[0])
+    own_q.start()
+    kv_place = pl.ds(pl.multiple_of(z * rows, rows), rows)
+    own_kv = pltpu.make_async_copy(kv_ref, kv_all.at[kv_place], own_sem.at[1])
+    own_kv.start()
+    for step in range(2, 5):
+        for chunk in range(2):
+            for way in range(2):
+                ring[way, step - 1, chunk].wait_recv()
+                if step < 4 or chunk == way:
+                    ring[way, step, chunk] = ring_copy(way, step, chunk)
+                    ring[way, step, chunk].start()
+    for way in range(2):
+        ring[way, 4, way].wait_recv()
+    for copy in ring.values():
+        copy.wait_send()
+    for push in pushes:
+        push.wait_send()
+        push.wait_recv()
+    own_q.wait()
+    own_kv.wait()
+
+
+def gather_both(queries, kv):
+    rows, inner = queries.shape
+    hbm = pl.BlockSpec(memory_space=pl.ANY)
+    return pl.pallas_call(
+        gather_kernel,
+        in_specs=[hbm, hbm],
+        out_specs=[hbm, hbm],
+        out_shape=[
+            jax.ShapeDtypeStruct((8 * rows, inner), jnp.bfloat16),
+            jax.ShapeDtypeStruct((8 * rows, 2 * inner), jnp.bfloat16),
+        ],
+        scratch_shapes=[
+            pltpu.SemaphoreType.DMA((8,)),
+            pltpu.SemaphoreType.DMA((8,)),
+            pltpu.SemaphoreType.DMA((2, 4, 2)),
+            pltpu.SemaphoreType.DMA((2, 4, 2)),
+            pltpu.SemaphoreType.DMA((2,)),
+        ],
+        compiler_params=pltpu.CompilerParams(collective_id=0, has_side_effects=True),
+    )(queries, kv)
+
+
 Z_SIZE = 8
-KV_GROUPS = [[y * 16 + z * 2 + x for z in range(8)] for y in range(4) for x in range(2)]
 Q_GROUPS = [[y * 16 + z * 2 + x for y in range(4) for x in range(2)] for z in range(8)]
 
 
@@ -136,8 +233,7 @@
     head_size = inner // HEADS
     queries = to_bf16(projected[:, :inner] * head_size ** (-0.5))
     kv = to_bf16(projected[:, inner:])
-    kv_all = lax.all_gather(kv, "ctx", axis=0, tiled=True, axis_index_groups=KV_GROUPS)
-    q_all = lax.all_gather(queries, "ctx", axis=0, tiled=True, axis_index_groups=Q_GROUPS)
+    q_all, kv_all = gather_both(queries, kv)
     group_start = (my_index // 16) * 16 + my_index % 2
     key_rows = jnp.arange(Z_SIZE * frame_rows, dtype=jnp.int32)
     key_spots = (group_start + 2 * (key_rows // frame_rows)) * frame_rows + key_rows % frame_rows

time: 207 us -> 139 us (0.67)
  waiting for transfers between devices: 117 us -> 24 us
  Pallas kernels: 28.9 us -> 69.1 us
  between operations: 14.3 us -> 0.85 us
  local copies, waits for them, and re-layouts: 10.9 us -> 8.73 us
    all_gather x2 -> x0, waiting for transfers between devices: 92 us -> none  [the longest x1 48.1 us: per_device(): lax.all_gather(kv, 'ctx', axis=0, tiled=True, axis_index_groups=KV_GROUPS)]
    pallas_call x0 -> x1, Pallas kernels: none -> 40.2 us  [gather_both(): pl.pallas_call(gather_kernel, in_specs=[hbm, hbm], out_specs=[hbm, hbm],...]
    unnamed x13 -> x11, local copies, waits for them, and re-layouts: 4.74 us -> 3.73 us
  transfers between devices with their start and end apart: 5 -> 3, of which waited for: 4 -> 2; matrix products, arithmetic and copies ran while one was open for 1% -> 0% of each run, Pallas kernels for 0% -> 0%
where the time goes in v2:
time: 139 us; the launch traced here: 138 us
  Pallas kernels  69.1 us (50%)
  waiting for transfers between devices  24 us (17%)
  other arithmetic  15.2 us (11%)
  starting transfers between devices  14.7 us (11%)
  local copies, waits for them, and re-layouts  8.73 us (6%)
  matrix products  5.46 us (4%)
    pallas_call x1, Pallas kernels, gather_both(): pl.pallas_call(gather_kernel, in_specs=[hbm, hbm], out_specs=[hbm, hbm],...  40.2 us
    pallas_call x1, Pallas kernels, attend(): pl.pallas_call(attend_kernel, grid=(count // block,), in_specs=[pl.BlockS...  28.9 us
    all_to_all x1, waiting for transfers between devices, per_device(): lax.all_to_all(partial, 'ctx', split_axis=0, concat_axis=0, tiled=True, a...  22.5 us
    reduce_sum x2, other arithmetic, layer_norm(): center = value - jnp.mean(value, axis=-1, keepdims=True)  5.78 us
    all_to_all x1, starting transfers between devices, per_device(): lax.all_to_all(partial, 'ctx', split_axis=0, concat_axis=0, tiled=True, a...  5.68 us
    ppermute x1, starting transfers between devices, padded_2(): lax.ppermute(head, axis, [((i + 1) % count, i) for i in range(ends)])  5.48 us
    unnamed x11, local copies, waits for them, and re-layouts  3.73 us
    ppermute x1, starting transfers between devices, padded_2(): lax.ppermute(tail, axis, [(i, (i + 1) % count) for i in range(ends)])  3.5 us
  transfers between devices with their start and end apart: 3, of which 2 were waited for; matrix products, arithmetic and copies ran while one was open for 0% of the time, Pallas kernels for 0%

profile of v2, /device:TPU:8, one launch (start us, length us, event | category | flops | bytes accessed | tf_op | source)
XLA Modules:
  0.0 138.0 jit_solution(11348046156129640676)
XLA Ops:
  0.0 1.3 convert_reduce_fusion
  1.3 1.2 fusion.6
  2.6 1.8 %fusion.18 = f32[192,1536]{1,0:T(8,128)S(1)} fusion(bf16[1024,1536]{1,0:T(8,128)(2,1)S(1)} %copy-done, bf16[1,192,1024]{2,1,0:T(8,128)(2,1)} %param.7, f32[192]{0:T(256)S(1)} %add_rsqrt_fusion.3, f32[192]{0:T(256)S(1)} %broadcast_multiply_fusion.3), kind=kOutput, calls=%fused_computation.63 | convolution fusion | flops 604766208 | bytes 4720128 | tf_op jit(solution)/shard_map/dot_general | solution.py:231
  4.4 0.8 slice.616.kv_ref
  5.2 0.7 fusion.48.q_ref
  6.6 0.6 compare_select_fusion.bias_ref
  7.2 40.2 %shard_map.73 = (bf16[1536,512]{1,0:T(8,128)(2,1)}, bf16[1536,1024]{1,0:T(8,128)(2,1)}) custom-call(bf16[192,512]{1,0:T(8,128)(2,1)} %fusion.48.q_ref, bf16[192,1024]{1,0:T(8,128)(2,1)} %slice.616.kv_ref), custom_call_target="tpu_custom_call" | custom-call | tf_op jit(solution)/shard_map/pallas_call | solution.py:199
  47.4 28.9 %shard_map.74 = bf16[1536,640]{1,0:T(8,128)(2,1)} custom-call(f32[1,1536]{1,0:T(1,128)} %compare_select_fusion.bias_ref, bf16[1536,512]{1,0:T(8,128)(2,1)} %get-tuple-element.7.q_ref, bf16[1536,1024]{1,0:T(8,128)(2,1)} %get-tuple-element.8.kv_ref), custom_call_target="tpu_custom_call" | custom-call | tf_op jit(solution)/shard_map/pallas_call | solution.py:106
  76.3 5.7 %all-to-all-start = ((bf16[8,192,640]{2,1,0:T(8,128)(2,1)}), bf16[8,192,640]{2,1,0:T(8,128)(2,1)}, u32[]{:S(2)}, u32[]{:S(2)}) async-start(bf16[8,192,640]{2,1,0:T(8,128)(2,1)} %bitcast.61), calls=%async_computation | async-start | bytes 3932160 | tf_op jit(solution)/shard_map/all_to_all | solution.py:243
  82.1 22.5 %all-to-all-done = bf16[8,192,640]{2,1,0:T(8,128)(2,1)} async-done(((bf16[8,192,640]{2,1,0:T(8,128)(2,1)}), bf16[8,192,640]{2,1,0:T(8,128)(2,1)}, u32[]{:S(2)}, u32[]{:S(2)}) %all-to-all-start) | async-done | bytes 1966112 | tf_op jit(solution)/shard_map/all_to_all | solution.py:243
  104.6 1.0 slice_convert_fusion.1
  106.3 1.0 fusion.14
  107.3 1.4 %copy.10 = f32[8,192,8]{1,2,0:T(8,128)S(1)} copy(f32[8,192,8]{2,1,0:T(8,128)} %fusion.14) | data formatting | bytes 98304 | tf_op jit(solution)/shard_map/div | solution.py:249
  108.7 2.7 %slice.321 = bf16[8,192,512]{2,1,0:T(8,128)(2,1)} slice(bf16[8,192,640]{2,1,0:T(8,128)(2,1)} %all-to-all-done), slice={[0:8], [0:192], [0:512]} | slice | bytes 3145728 | tf_op jit(solution)/shard_map/slice | solution.py:251
  111.4 3.7 %copy.11 = bf16[8,192,512]{1,2,0:T(8,128)(2,1)} copy(bf16[8,192,512]{2,1,0:T(8,128)(2,1)} %slice.321) | data formatting | bytes 3145728
  115.1 2.2 %fusion = bf16[192,512]{0,1:T(8,128)(2,1)S(1)} fusion(bf16[8,192,512]{1,2,0:T(8,128)(2,1)} %copy.11, f32[8,192,8]{1,2,0:T(8,128)S(1)} %copy.10), kind=kLoop, calls=%fused_computation.1 | loop fusion | flops 2260992 | bytes 1818624 | tf_op jit(solution)/shard_map/reduce_sum | solution.py:251
  117.3 1.7 %fusion.67 = (f32[192]{0:T(256)S(1)}, f32[192,1024]{1,0:T(8,128)S(1)}) fusion(bf16[192,512]{0,1:T(8,128)(2,1)S(1)} %fusion, bf16[512,1024]{1,0:T(8,128)(2,1)} %param.10, bf16[1,192,1024]{2,1,0:T(8,128)(2,1)S(1)} %copy-done.1), kind=kOutput, calls=%fused_computation.148 | convolution fusion | flops 202309440 | bytes 2425600 | tf_op jit(solution)/shard_map/dot_general | solution.py:253
  119.3 1.1 fusion.16
  120.6 3.5 %collective-permute-start = (bf16[15,1024]{1,0:T(8,128)(2,1)S(1)}, bf16[15,1024]{1,0:T(8,128)(2,1)S(1)}, u32[]{:S(2)}, u32[]{:S(2)}) collective-permute-start(bf16[15,1024]{1,0:T(8,128)(2,1)S(1)} %get-tuple-element.13), channel_id=1, source_target_pairs={{0,1},{1,2},{2,3},{3,4},{4,5},{5,6},{6,7},{7,8},{8,9},{9,10},{10,1... | collective-permute-start | bytes 92168 | tf_op jit(solution)/shard_map/ppermute | solution.py:23
  124.1 5.5 %collective-permute-start.1 = (bf16[15,1024]{1,0:T(8,128)(2,1)S(1)}, bf16[15,1024]{1,0:T(8,128)(2,1)S(1)}, u32[]{:S(2)}, u32[]{:S(2)}) collective-permute-start(bf16[15,1024]{1,0:T(8,128)(2,1)S(1)} %get-tuple-element.14), channel_id=1, source_target_pairs={{1,0},{2,1},{3,2},{4,3},{5,4},{6,5},{7,6},{8,7},{9,8},{10,9},{11,1... | collective-permute-start | bytes 92168 | tf_op jit(solution)/shard_map/ppermute | solution.py:25
  129.7 1.5 %collective-permute-done.1 = bf16[15,1024]{1,0:T(8,128)(2,1)S(1)} collective-permute-done((bf16[15,1024]{1,0:T(8,128)(2,1)S(1)}, bf16[15,1024]{1,0:T(8,128)(2,1)S(1)}, u32[]{:S(2)}, u32[]{:S(2)}) %collective-permute-start.1) | collective-permute-done | bytes 30752 | tf_op jit(solution)/shard_map/ppermute | solution.py:25
  131.2 4.5 %fusion.62 = (f32[192]{0:T(256)S(1)}, f32[192,1024]{1,0:T(8,128)S(1)}) fusion(bf16[15,1024]{1,0:T(8,128)(2,1)S(1)} %collective-permute-done.1, bf16[192,1024]{1,0:T(8,128)(2,1)S(1)} %fusion.13, f32[1024]{0:T(1024)S(1)} %bitcast.91, f32[1024]{0:T(1024)S(1)} %bitcast.92, f32[1024]{0:T(1024)S(1)} %bitcast.63, f32[1024]{0:T(1024)S(1)} %bitcast.64, ...), kind=kLoop, calls=%fused_computation.143 | loop fusion | flops 35979072 | bytes 1368832 | tf_op jit(solution)/shard_map/reduce_sum | solution.py:37
  136.0 0.8 fusion.68
  137.1 0.9 fusion.17
  (29 shorter events, 1.7 us)
Async XLA Ops:
  0.0 2.5 %copy-start = (bf16[1024,1536]{1,0:T(8,128)(2,1)S(1)}, bf16[1024,1536]{1,0:T(8,128)(2,1)}, u32[]{:S(2)}) copy-start(bf16[1024,1536]{1,0:T(8,128)(2,1)} %param.9) | copy-start | bytes 9437188
  76.3 5.7 %copy-start.3 = (f32[31,1024]{1,0:T(8,128)S(1)}, f32[31,1024]{1,0:T(8,128)}, u32[]{:S(2)}) copy-start(f32[31,1024]{1,0:T(8,128)} %param.12) | copy-start | bytes 380932
  76.3 28.3 %all-to-all-start = ((bf16[8,192,640]{2,1,0:T(8,128)(2,1)}), bf16[8,192,640]{2,1,0:T(8,128)(2,1)}, u32[]{:S(2)}, u32[]{:S(2)}) async-start(bf16[8,192,640]{2,1,0:T(8,128)(2,1)} %bitcast.61), calls=%async_computation | async-start | bytes 3932160 | tf_op jit(solution)/shard_map/all_to_all | solution.py:243
  115.1 2.2 %copy-start.1 = (bf16[1,192,1024]{2,1,0:T(8,128)(2,1)S(1)}, bf16[1,192,1024]{2,1,0:T(8,128)(2,1)}, u32[]{:S(2)}) copy-start(bf16[1,192,1024]{2,1,0:T(8,128)(2,1)} %param.7) | copy-start | bytes 1179652
  115.1 4.2 %copy-start.2 = (bf16[1024,2048]{1,0:T(8,128)(2,1)S(1)}, bf16[1024,2048]{1,0:T(8,128)(2,1)}, u32[]{:S(2)}) copy-start(bf16[1024,2048]{1,0:T(8,128)(2,1)} %param.11) | copy-start | bytes 12582916
  120.4 15.6 %copy-start.4 = (bf16[1024,1024]{1,0:T(8,128)(2,1)S(1)}, bf16[1024,1024]{1,0:T(8,128)(2,1)}, u32[]{:S(2)}) copy-start(bf16[1024,1024]{1,0:T(8,128)(2,1)} %param.13) | copy-start | bytes 6291460
  120.6 9.0 %collective-permute-start = (bf16[15,1024]{1,0:T(8,128)(2,1)S(1)}, bf16[15,1024]{1,0:T(8,128)(2,1)S(1)}, u32[]{:S(2)}, u32[]{:S(2)}) collective-permute-start(bf16[15,1024]{1,0:T(8,128)(2,1)S(1)} %get-tuple-element.13), channel_id=1, source_target_pairs={{0,1},{1,2},{2,3},{3,4},{4,5},{5,6},{6,7},{7,8},{8,9},{9,10},{10,1... | collective-permute-start | bytes 92168 | tf_op jit(solution)/shard_map/ppermute | solution.py:23
  124.1 7.1 %collective-permute-start.1 = (bf16[15,1024]{1,0:T(8,128)(2,1)S(1)}, bf16[15,1024]{1,0:T(8,128)(2,1)S(1)}, u32[]{:S(2)}, u32[]{:S(2)}) collective-permute-start(bf16[15,1024]{1,0:T(8,128)(2,1)S(1)} %get-tuple-element.14), channel_id=1, source_target_pairs={{1,0},{2,1},{3,2},{4,3},{5,4},{6,5},{7,6},{8,7},{9,8},{10,9},{11,1... | collective-permute-start | bytes 92168 | tf_op jit(solution)/shard_map/ppermute | solution.py:25

commit v3 on v2

--- a/solution.py
+++ b/solution.py
@@ -59,7 +59,7 @@
     return to_bf16(jnp.where((spots < limit)[:, None], result, 0.0))
 
 
-def attend_kernel(bias_ref, q_ref, kv_ref, out_ref):
+def attend_rows(bias_ref, q_ref, kv_ref, out_ref):
     rows = q_ref.shape[0]
     inner = q_ref.shape[1]
     keys = kv_ref.shape[0]
@@ -99,21 +99,80 @@
     out_ref[:, inner:] = packed.astype(jnp.bfloat16)
 
 
+def attend_kernel(bias_ref, q_ref, kv_ref, back_ref, held, send_sem, recv_sem, own_sem):
+    step = pl.program_id(0)
+    me = lax.axis_index("ctx")
+    y, z, x = me // 16, (me // 2) % 8, me % 2
+    mine = y * 2 + x
+    rows = back_ref.shape[0] // 8
+
+    @pl.when(step == 0)
+    def _():
+        barrier = pltpu.get_barrier_semaphore()
+        for j in range(1, 8):
+            spot = lax.rem(mine + j, 8)
+            peer = (spot // 2) * 16 + z * 2 + lax.rem(spot, 2)
+            pl.semaphore_signal(
+                barrier, inc=1, device_id={"ctx": peer}, device_id_type=pl.DeviceIdType.MESH
+            )
+        pl.semaphore_wait(barrier, 7)
+
+    to_y = lax.rem(y + 1 + step, 4)
+    q_rows = q_ref.at[pl.ds(pl.multiple_of(to_y * 2 * rows, 2 * rows), 2 * rows)]
+    attend_rows(bias_ref, q_rows, kv_ref, held.at[step])
+    place = pl.ds(pl.multiple_of(mine * rows, rows), rows)
+
+    def push(at_step, to_x, flip):
+        return pltpu.make_async_remote_copy(
+            src_ref=held.at[at_step, pl.ds(pl.multiple_of(to_x * rows, rows), rows)],
+            dst_ref=back_ref.at[place],
+            send_sem=send_sem.at[at_step, flip],
+            recv_sem=recv_sem.at[at_step, flip],
+            device_id={"ctx": lax.rem(y + 1 + at_step, 4) * 16 + z * 2 + to_x},
+            device_id_type=pl.DeviceIdType.MESH,
+        )
+
+    push(step, 1 - x, 1).start()
+
+    @pl.when(step < 3)
+    def _():
+        push(step, x, 0).start()
+
+    @pl.when(step == 3)
+    def _():
+        own = pltpu.make_async_copy(
+            held.at[3, pl.ds(pl.multiple_of(x * rows, rows), rows)], back_ref.at[place], own_sem
+        )
+        own.start()
+        for k in range(4):
+            push(k, 1 - x, 1).wait()
+            if k < 3:
+                push(k, x, 0).wait()
+        own.wait()
+
+
 def attend(bias, queries, kv):
     count, inner = queries.shape
     keys = kv.shape[0]
-    block = 512
     return pl.pallas_call(
         attend_kernel,
-        grid=(count // block,),
+        grid=(4,),
         in_specs=[
             pl.BlockSpec((1, keys), lambda i: (0, 0)),
-            pl.BlockSpec((block, inner), lambda i: (i, 0)),
+            pl.BlockSpec((count, inner), lambda i: (0, 0)),
             pl.BlockSpec((keys, 2 * inner), lambda i: (0, 0)),
         ],
-        out_specs=pl.BlockSpec((block, inner + 128), lambda i: (i, 0)),
+        out_specs=pl.BlockSpec(memory_space=pl.ANY),
         out_shape=jax.ShapeDtypeStruct((count, inner + 128), jnp.bfloat16),
-        compiler_params=pltpu.CompilerParams(vmem_limit_bytes=60 * 1024 * 1024),
+        scratch_shapes=[
+            pltpu.VMEM((4, count // 4, inner + 128), jnp.bfloat16),
+            pltpu.SemaphoreType.DMA((4, 2)),
+            pltpu.SemaphoreType.DMA((4, 2)),
+            pltpu.SemaphoreType.DMA,
+        ],
+        compiler_params=pltpu.CompilerParams(
+            collective_id=1, has_side_effects=True, vmem_limit_bytes=60 * 1024 * 1024
+        ),
     )(bias, queries, kv)
 
 
@@ -216,7 +275,6 @@
 
 
 Z_SIZE = 8
-Q_GROUPS = [[y * 16 + z * 2 + x for y in range(4) for x in range(2)] for z in range(8)]
 
 
 def per_device(frames, lengths, w_qkv, w_out, w_pw1, conv_taps, w_pw2):
@@ -238,11 +296,8 @@
     key_rows = jnp.arange(Z_SIZE * frame_rows, dtype=jnp.int32)
     key_spots = (group_start + 2 * (key_rows // frame_rows)) * frame_rows + key_rows % frame_rows
     bias = jnp.where(key_spots < limit, 0.0, masked_score).astype(jnp.float32)[None]
-    partial = attend(bias, q_all, kv_all)
-    width = partial.shape[1]
-    returned = lax.all_to_all(
-        partial, "ctx", split_axis=0, concat_axis=0, tiled=True, axis_index_groups=Q_GROUPS
-    ).reshape(8, frame_rows, width)
+    returned = attend(bias, q_all, kv_all)
+    returned = returned.reshape(8, frame_rows, returned.shape[1])
     stats = returned[:, :, inner : inner + 24].astype(jnp.float32)
     lse = stats[:, :, 0:8] + stats[:, :, 8:16] + stats[:, :, 16:24]
     share = jnp.exp(lse - jnp.max(lse, axis=0))

time: 139 us -> 123 us (0.88)
  waiting for transfers between devices: 24 us -> 1.45 us
  Pallas kernels: 69.1 us -> 79.8 us
  starting transfers between devices: 14.7 us -> 8.98 us
    all_to_all x1 -> x0, waiting for transfers between devices: 22.5 us -> none  [per_device(): lax.all_to_all(partial, 'ctx', split_axis=0, concat_axis=0, tiled=True, a...]
    pallas_call x1, Pallas kernels: 28.9 us -> 39.6 us  [attend(): pl.pallas_call(attend_kernel, grid=(4,), in_specs=[pl.BlockSpec((1, keys)...]
    all_to_all x1 -> x0, starting transfers between devices: 5.68 us -> none  [per_device(): lax.all_to_all(partial, 'ctx', split_axis=0, concat_axis=0, tiled=True, a...]
    dot_general x1, matrix products: 1.06 us -> 3.48 us  [gate_rows(): jnp.dot(to_bf16(layer_norm(stream_rows.astype(jnp.float32))), w_pw1, pref...]
    unnamed x11 -> x15, local copies, waits for them, and re-layouts: 3.73 us -> 4.62 us
  transfers between devices with their start and end apart: 3 -> 2, of which waited for: 2 -> 1; matrix products, arithmetic and copies ran while one was open for 0% -> 0% of each run, Pallas kernels for 0% -> 0%
where the time goes in v3:
time: 123 us; the launch traced here: 122 us
  Pallas kernels  79.8 us (65%)
  other arithmetic  15.1 us (12%)
  local copies, waits for them, and re-layouts  9.64 us (8%)
  starting transfers between devices  8.98 us (7%)
  matrix products  6.66 us (5%)
  waiting for transfers between devices  1.45 us (1%)
    pallas_call x1, Pallas kernels, gather_both(): pl.pallas_call(gather_kernel, in_specs=[hbm, hbm], out_specs=[hbm, hbm],...  40.2 us
    pallas_call x1, Pallas kernels, attend(): pl.pallas_call(attend_kernel, grid=(4,), in_specs=[pl.BlockSpec((1, keys)...  39.6 us
    reduce_sum x2, other arithmetic, layer_norm(): center = value - jnp.mean(value, axis=-1, keepdims=True)  5.77 us
    ppermute x1, starting transfers between devices, padded_2(): lax.ppermute(head, axis, [((i + 1) % count, i) for i in range(ends)])  5.48 us
    unnamed x15, local copies, waits for them, and re-layouts  4.62 us
    ppermute x1, starting transfers between devices, padded_2(): lax.ppermute(tail, axis, [(i, (i + 1) % count) for i in range(ends)])  3.5 us
    dot_general x1, matrix products, gate_rows(): jnp.dot(to_bf16(layer_norm(stream_rows.astype(jnp.float32))), w_pw1, pref...  3.48 us
    slice x1, local copies, waits for them, and re-layouts, per_device(): returned[:, :, :inner].astype(jnp.float32) * share  2.69 us
  transfers between devices with their start and end apart: 2, of which 1 were waited for; matrix products, arithmetic and copies ran while one was open for 0% of the time, Pallas kernels for 0%

profile of v3, /device:TPU:8, one launch (start us, length us, event | category | flops | bytes accessed | tf_op | source)
XLA Modules:
  0.0 122.5 jit_solution(10737612715124712902)
XLA Ops:
  0.0 1.3 %convert_reduce_fusion = f32[192]{0:T(256)S(1)} fusion(bf16[1,192,1024]{2,1,0:T(8,128)(2,1)} %param.7), kind=kLoop, calls=%fused_computation.34 | loop fusion | flops 393024 | bytes 393984 | tf_op jit(solution)/shard_map/reduce_sum | solution.py:37
  1.3 1.2 %fusion.6 = f32[192]{0:T(256)S(1)} fusion(bf16[1,192,1024]{2,1,0:T(8,128)(2,1)} %param.7, f32[192]{0:T(256)S(1)} %broadcast_multiply_fusion.3), kind=kLoop, calls=%fused_computation.39 | loop fusion | flops 786240 | bytes 394752 | tf_op jit(solution)/shard_map/reduce_sum | solution.py:38
  2.6 1.8 %fusion.18 = f32[192,1536]{1,0:T(8,128)S(1)} fusion(bf16[1024,1536]{1,0:T(8,128)(2,1)S(1)} %copy-done, bf16[1,192,1024]{2,1,0:T(8,128)(2,1)} %param.7, f32[192]{0:T(256)S(1)} %add_rsqrt_fusion.3, f32[192]{0:T(256)S(1)} %broadcast_multiply_fusion.3), kind=kOutput, calls=%fused_computation.63 | convolution fusion | flops 604766208 | bytes 4720128 | tf_op jit(solution)/shard_map/dot_general | solution.py:289
  4.4 0.8 slice.616.kv_ref
  5.2 0.7 fusion.48.q_ref
  6.6 0.6 compare_select_fusion.bias_ref
  7.2 40.2 %shard_map.73 = (bf16[1536,512]{1,0:T(8,128)(2,1)}, bf16[1536,1024]{1,0:T(8,128)(2,1)}) custom-call(bf16[192,512]{1,0:T(8,128)(2,1)} %fusion.48.q_ref, bf16[192,1024]{1,0:T(8,128)(2,1)} %slice.616.kv_ref), custom_call_target="tpu_custom_call" | custom-call | tf_op jit(solution)/shard_map/pallas_call | solution.py:258
  47.4 39.6 %shard_map.74 = bf16[1536,640]{1,0:T(8,128)(2,1)} custom-call(f32[1,1536]{1,0:T(1,128)} %compare_select_fusion.bias_ref, bf16[1536,512]{1,0:T(8,128)(2,1)} %get-tuple-element.7.q_ref, bf16[1536,1024]{1,0:T(8,128)(2,1)} %get-tuple-element.8.kv_ref), custom_call_target="tpu_custom_call" | custom-call | tf_op jit(solution)/shard_map/pallas_call | solution.py:157
  87.0 1.0 slice_convert_fusion.1
  88.0 2.7 %slice.321 = bf16[8,192,512]{2,1,0:T(8,128)(2,1)} slice(bf16[8,192,640]{2,1,0:T(8,128)(2,1)} %bitcast.62), slice={[0:8], [0:192], [0:512]} | slice | bytes 3145728 | tf_op jit(solution)/shard_map/slice | solution.py:306
  90.7 0.5 fusion.63
  91.3 1.0 fusion.14
  92.3 1.4 %copy.11 = f32[8,192,8]{1,2,0:T(8,128)S(1)} copy(f32[8,192,8]{2,1,0:T(8,128)} %fusion.14) | data formatting | bytes 98304 | tf_op jit(solution)/shard_map/div | solution.py:304
  93.8 3.7 %copy.12 = bf16[8,192,512]{1,2,0:T(8,128)(2,1)} copy(bf16[8,192,512]{2,1,0:T(8,128)(2,1)} %slice.321) | data formatting | bytes 3145728
  97.5 2.2 %fusion = bf16[192,512]{0,1:T(8,128)(2,1)S(1)} fusion(bf16[8,192,512]{1,2,0:T(8,128)(2,1)} %copy.12, f32[8,192,8]{1,2,0:T(8,128)S(1)} %copy.11), kind=kLoop, calls=%fused_computation.1 | loop fusion | flops 2260992 | bytes 1818624 | tf_op jit(solution)/shard_map/reduce_sum | solution.py:306
  99.7 0.5 fusion.67
  100.2 0.9 copy-done.1
  101.3 3.5 %fusion.16 = f32[192,2048]{1,0:T(8,128)S(1)} fusion(bf16[1024,2048]{1,0:T(8,128)(2,1)} %param.11, f32[192,1024]{1,0:T(8,128)} %copy-done.1, f32[192]{0:T(256)S(1)} %add_rsqrt_fusion.2, f32[192]{0:T(256)S(1)} %broadcast_multiply_fusion.2), kind=kOutput, calls=%fused_computation.61 | convolution fusion | flops 805896192 | bytes 6555136 | tf_op jit(solution)/shard_map/dot_general | solution.py:52
  105.1 3.5 %collective-permute-start = (bf16[15,1024]{1,0:T(8,128)(2,1)S(1)}, bf16[15,1024]{1,0:T(8,128)(2,1)S(1)}, u32[]{:S(2)}, u32[]{:S(2)}) collective-permute-start(bf16[15,1024]{1,0:T(8,128)(2,1)S(1)} %get-tuple-element.13), channel_id=1, source_target_pairs={{0,1},{1,2},{2,3},{3,4},{4,5},{5,6},{6,7},{7,8},{8,9},{9,10},{10,1... | collective-permute-start | bytes 92168 | tf_op jit(solution)/shard_map/ppermute | solution.py:23
  108.6 5.5 %collective-permute-start.1 = (bf16[15,1024]{1,0:T(8,128)(2,1)S(1)}, bf16[15,1024]{1,0:T(8,128)(2,1)S(1)}, u32[]{:S(2)}, u32[]{:S(2)}) collective-permute-start(bf16[15,1024]{1,0:T(8,128)(2,1)S(1)} %get-tuple-element.14), channel_id=1, source_target_pairs={{1,0},{2,1},{3,2},{4,3},{5,4},{6,5},{7,6},{8,7},{9,8},{10,9},{11,1... | collective-permute-start | bytes 92168 | tf_op jit(solution)/shard_map/ppermute | solution.py:25
  114.3 1.4 %collective-permute-done.1 = bf16[15,1024]{1,0:T(8,128)(2,1)S(1)} collective-permute-done((bf16[15,1024]{1,0:T(8,128)(2,1)S(1)}, bf16[15,1024]{1,0:T(8,128)(2,1)S(1)}, u32[]{:S(2)}, u32[]{:S(2)}) %collective-permute-start.1) | collective-permute-done | bytes 30752 | tf_op jit(solution)/shard_map/ppermute | solution.py:25
  115.7 4.5 %fusion.62 = (f32[192]{0:T(256)S(1)}, f32[192,1024]{1,0:T(8,128)S(1)}) fusion(bf16[15,1024]{1,0:T(8,128)(2,1)S(1)} %collective-permute-done.1, bf16[192,1024]{1,0:T(8,128)(2,1)S(1)} %fusion.13, f32[1024]{0:T(1024)S(1)} %bitcast.92, f32[1024]{0:T(1024)S(1)} %bitcast.93, f32[1024]{0:T(1024)S(1)} %bitcast.64, f32[1024]{0:T(1024)S(1)} %bitcast.65, ...), kind=kLoop, calls=%fused_computation.143 | loop fusion | flops 35979072 | bytes 1368832 | tf_op jit(solution)/shard_map/reduce_sum | solution.py:37
  120.5 0.8 fusion.68
  121.6 0.9 fusion.17
  (31 shorter events, 1.3 us)
Async XLA Ops:
  0.0 2.5 %copy-start = (bf16[1024,1536]{1,0:T(8,128)(2,1)S(1)}, bf16[1024,1536]{1,0:T(8,128)(2,1)}, u32[]{:S(2)}) copy-start(bf16[1024,1536]{1,0:T(8,128)(2,1)} %param.9) | copy-start | bytes 9437188
  97.5 2.2 %copy-start.3 = (bf16[1,192,1024]{2,1,0:T(8,128)(2,1)S(1)}, bf16[1,192,1024]{2,1,0:T(8,128)(2,1)}, u32[]{:S(2)}) copy-start(bf16[1,192,1024]{2,1,0:T(8,128)(2,1)} %param.7) | copy-start | bytes 1179652
  97.5 2.2 %copy-start.4 = (bf16[512,1024]{1,0:T(8,128)(2,1)S(1)}, bf16[512,1024]{1,0:T(8,128)(2,1)}, u32[]{:S(2)}) copy-start(bf16[512,1024]{1,0:T(8,128)(2,1)} %param.10) | copy-start | bytes 3145732
  100.2 0.9 copy-start.1
  104.8 9.3 %copy-start.5 = (f32[31,1024]{1,0:T(8,128)S(1)}, f32[31,1024]{1,0:T(8,128)}, u32[]{:S(2)}) copy-start(f32[31,1024]{1,0:T(8,128)} %param.12) | copy-start | bytes 380932
  104.8 15.6 %copy-start.2 = (f32[192,1024]{1,0:T(8,128)S(1)}, f32[192,1024]{1,0:T(8,128)}, u32[]{:S(2)}) copy-start(f32[192,1024]{1,0:T(8,128)} %copy-done.1) | copy-start | bytes 2359300
  104.9 15.6 %copy-start.6 = (bf16[1024,1024]{1,0:T(8,128)(2,1)S(1)}, bf16[1024,1024]{1,0:T(8,128)(2,1)}, u32[]{:S(2)}) copy-start(bf16[1024,1024]{1,0:T(8,128)(2,1)} %param.13) | copy-start | bytes 6291460
  105.1 9.1 %collective-permute-start = (bf16[15,1024]{1,0:T(8,128)(2,1)S(1)}, bf16[15,1024]{1,0:T(8,128)(2,1)S(1)}, u32[]{:S(2)}, u32[]{:S(2)}) collective-permute-start(bf16[15,1024]{1,0:T(8,128)(2,1)S(1)} %get-tuple-element.13), channel_id=1, source_target_pairs={{0,1},{1,2},{2,3},{3,4},{4,5},{5,6},{6,7},{7,8},{8,9},{9,10},{10,1... | collective-permute-start | bytes 92168 | tf_op jit(solution)/shard_map/ppermute | solution.py:23
  108.6 7.1 %collective-permute-start.1 = (bf16[15,1024]{1,0:T(8,128)(2,1)S(1)}, bf16[15,1024]{1,0:T(8,128)(2,1)S(1)}, u32[]{:S(2)}, u32[]{:S(2)}) collective-permute-start(bf16[15,1024]{1,0:T(8,128)(2,1)S(1)} %get-tuple-element.14), channel_id=1, source_target_pairs={{1,0},{2,1},{3,2},{4,3},{5,4},{6,5},{7,6},{8,7},{9,8},{10,9},{11,1... | collective-permute-start | bytes 92168 | tf_op jit(solution)/shard_map/ppermute | solution.py:25
